TPU v7x, 32 devices: a whole 2x2x4 slice. The times are simulated.
32 devices in a mesh: member: 8 (over y, x, core), lat: 4 (over z).
Axes of the slice: x: 2, y: 2, z: 4, core: 2. Of those that a mesh axis runs over, the one named last changes fastest.
Arguments:
- state: float32 [32, 32, 8, 256], P('member', 'lat'), may hold values from -6 to 6
- zonal_wind: float32 [32, 8, 256], P('lat'), may hold values from -5 to 5
- meridional_wind: float32 [32, 8, 256], P('lat'), may hold values from -5 to 5
- obs_cell: int32 [32, 8, 128], P('lat'), may hold values from 0 to 255
- obs_value: float32 [32, 8, 128], P('lat'), may hold values from -10 to 10
- obs_weight: float32 [32, 8, 128], P('lat'), may hold values from 1 to 1024
Outputs:
- analysis: float32 [32, 32, 8, 256], P('member', 'lat')
All inputs are finite; a program needn't handle non-finite values.
Results may differ from a plain program's by a relative error of at most 0.00014.
Values sent between devices are 32-bit elements; how exact they have to be, the bound alone decides.
No kernel may reach another device: no remote copies, remote signals or barrier semaphores. Data moves between devices by JAX's collectives and lax.ppermute only.
A program may use at most 64 MiB of HBM per device.

v0:
```python
import jax
import jax.numpy as jnp
from jax import lax
from jax.sharding import PartitionSpec as P

SWEEPS = 3
step_size = 0.3


def extended_2(block, sides, width):
    for axis, dim in sides:
        count = lax.axis_size(axis)
        forward = [(i, i + 1) for i in range(count - 1)]
        backward = [(target, source) for source, target in forward]
        low = lax.ppermute(
            lax.slice_in_dim(block, block.shape[dim] - width, None, axis=dim), axis, forward
        )
        high = lax.ppermute(lax.slice_in_dim(block, 0, width, axis=dim), axis, backward)
        block = jnp.concatenate([low, block, high], axis=dim)
    return block


def advance(padded, zonal, meridional):
    middle = padded[:, 1:-1]
    north_row = padded[:, 2:]
    south_row = padded[:, :-2]
    east_cell = jnp.roll(middle, -1, axis=3)
    west_cell = jnp.roll(middle, 1, axis=3)
    return middle - step_size * (
        (zonal + middle) * (east_cell - west_cell) * 0.5
        + meridional * (north_row - south_row) * 0.5
    )


def analyse(ensemble, observed, values, weights):
    highest = lax.Precision.HIGHEST
    count = ensemble.shape[0]
    obs_mean = jnp.mean(observed, axis=0)
    perturb = observed - obs_mean
    innovation = values - obs_mean
    gram = jnp.einsum("kro,lro->rkl", perturb * weights, perturb, precision=highest)
    identity = jnp.eye(count, dtype=jnp.float32)
    system = gram + (count - 1.0) * identity
    frobenius = jnp.sqrt(jnp.sum(system * system, axis=(1, 2)))
    iterate = system / frobenius[:, None, None]
    inverse = jnp.broadcast_to(identity, system.shape)
    for sweep in range(SWEEPS):
        product = jnp.einsum("rij,rjk->rik", inverse, iterate, precision=highest)
        factor = 1.5 * identity - 0.5 * product
        iterate = jnp.einsum("rij,rjk->rik", iterate, factor, precision=highest)
        inverse = jnp.einsum("rij,rjk->rik", factor, inverse, precision=highest)
    root = inverse / jnp.sqrt(frobenius)[:, None, None]
    covariance = jnp.einsum("rij,rjk->rik", root, root, precision=highest)
    projected = jnp.einsum("kro,ro->rk", perturb, weights * innovation, precision=highest)
    mean_weights = jnp.einsum("rkl,rl->rk", covariance, projected, precision=highest)
    transform = mean_weights[:, :, None] + jnp.sqrt(count - 1.0) * root
    state_mean = jnp.mean(ensemble, axis=0)
    state_pert = ensemble - state_mean
    return state_mean + jnp.einsum("rkm,krn->mrn", transform, state_pert, precision=highest)


def pick_columns(rows, cells):
    return jax.vmap(
        lambda block, index: jnp.take(block, index, axis=1), in_axes=(1, 0), out_axes=1
    )(rows, cells)


def body(state, zonal_wind, meridional_wind, obs_cell, obs_value, obs_weight):
    members_dev, lat_dev, levels, longitudes = state.shape
    groups = lax.axis_size("member")
    regions = lat_dev * levels // groups
    count = members_dev * groups
    stacked = jnp.concatenate([state, zonal_wind[None], meridional_wind[None]], axis=0)
    extended = extended_2(stacked, (("lat", 1),), 2)
    first = advance(
        extended[:members_dev], extended[members_dev, 1:-1], extended[members_dev + 1, 1:-1]
    )
    field = advance(first, zonal_wind, meridional_wind)
    flat = field.reshape(members_dev, lat_dev * levels, longitudes)
    all_cells = obs_cell.reshape(lat_dev * levels, -1)
    start = lax.axis_index("member") * regions
    cells = lax.dynamic_slice_in_dim(all_cells, start, regions, 0)
    values = lax.dynamic_slice_in_dim(obs_value.reshape(lat_dev * levels, -1), start, regions, 0)
    weights = lax.dynamic_slice_in_dim(obs_weight.reshape(lat_dev * levels, -1), start, regions, 0)
    ensemble = lax.all_to_all(
        flat.reshape(members_dev, groups, regions, longitudes),
        "member",
        split_axis=1,
        concat_axis=0,
        tiled=True,
    ).reshape(count, regions, longitudes)
    observed = pick_columns(ensemble, cells)
    analysed = analyse(ensemble, observed, values, weights)
    returned = lax.all_to_all(
        analysed.reshape(count, 1, regions, longitudes),
        "member",
        split_axis=0,
        concat_axis=1,
        tiled=True,
    )
    return returned.reshape(state.shape)


def solution(mesh):
    in_specs = (
        P("member", "lat", None, None),
        P("lat", None, None),
        P("lat", None, None),
        P("lat", None, None),
        P("lat", None, None),
        P("lat", None, None),
    )
    out_specs = P("member", "lat", None, None)
    return jax.shard_map(body, mesh=mesh, in_specs=in_specs, out_specs=out_specs, check_vma=False)
```

profile of v0, /device:TPU:0, one launch (start us, length us, event | category | flops | bytes accessed | tf_op | source)
XLA Modules:
  0.0 47.4 jit_solution(7783131057567353832)
XLA Ops:
  0.0 0.0 copy-start
  0.0 0.0 copy-start.1
  0.0 0.0 copy-start.2
  0.0 1.0 %pad_maximum_fusion.7 = (f32[6,2,8,256]{3,2,0,1:T(8,128)S(1)}, f32[6,2,8,256]{3,2,0,1:T(8,128)S(1)}) fusion(f32[1,8,8,256]{3,2,0,1:T(8,128)} %bitcast.75, f32[1,8,8,256]{3,2,0,1:T(8,128)} %bitcast.79, f32[4,8,8,256]{3,2,1,0:T(8,128)} %param.6), kind=kLoop, calls=%fused_computation.45 | loop fusion | flops 98304 | bytes 589824 | tf_op jit(solution)/shard_map/concatenate | solution.py:73
  1.0 5.0 %collective-permute-start = (f32[6,2,8,256]{3,2,0,1:T(8,128)S(1)}, f32[6,2,8,256]{3,2,0,1:T(8,128)S(1)}, u32[]{:S(2)}, u32[]{:S(2)}) collective-permute-start(f32[6,2,8,256]{3,2,0,1:T(8,128)S(1)} %get-tuple-element.12), channel_id=1, source_target_pairs={{0,1},{1,2},{2,3},{4,5},{5,6},{6,7},{8,9},{9,10},{10,11},{12,13},{... | collective-permute-start | bytes 294920 | tf_op jit(solution)/shard_map/ppermute | solution.py:15
  6.0 1.3 %collective-permute-start.1 = (f32[6,2,8,256]{3,2,0,1:T(8,128)S(1)}, f32[6,2,8,256]{3,2,0,1:T(8,128)S(1)}, u32[]{:S(2)}, u32[]{:S(2)}) collective-permute-start(f32[6,2,8,256]{3,2,0,1:T(8,128)S(1)} %get-tuple-element.11), channel_id=1, source_target_pairs={{1,0},{2,1},{3,2},{5,4},{6,5},{7,6},{9,8},{10,9},{11,10},{13,12},{... | collective-permute-start | bytes 294920 | tf_op jit(solution)/shard_map/ppermute | solution.py:18
  7.3 0.7 %fusion.37 = s32[1024]{0:T(1024)S(1)} fusion(s32[64,128]{1,0:T(8,128)} %bitcast.87, s32[]{:T(128)S(6)} %select_n.18), kind=kLoop, calls=%fused_computation.70 | loop fusion | flops 8192 | bytes 8196 | tf_op jit(solution)/shard_map/vmap(jit(_take))/gather | solution.py:64
  8.0 0.2 collective-permute-done
  8.2 4.3 %collective-permute-done.1 = f32[6,2,8,256]{3,2,0,1:T(8,128)S(1)} collective-permute-done((f32[6,2,8,256]{3,2,0,1:T(8,128)S(1)}, f32[6,2,8,256]{3,2,0,1:T(8,128)S(1)}, u32[]{:S(2)}, u32[]{:S(2)}) %collective-permute-start.1) | collective-permute-done | bytes 98336 | tf_op jit(solution)/shard_map/ppermute | solution.py:18
  12.5 0.0 copy-done
  12.5 0.0 copy-done.1
  12.5 0.0 copy-done.2
  12.6 0.2 fusion.42
  12.7 0.1 fusion.41
  12.9 0.2 fusion.8
  13.1 0.1 fusion.44
  13.3 0.1 fusion.43
  13.4 0.9 %fusion.13 = f32[4,8,8,256]{3,2,0,1:T(8,128)} fusion(f32[4,10,8,256]{3,2,0,1:T(8,128)S(1)} %fusion.8, f32[4,8,8,1]{3,2,0,1:T(8,128)S(1)} %get-tuple-element.14, f32[4,8,8,255]{3,2,0,1:T(8,128)S(1)} %get-tuple-element.16, f32[4,8,8,255]{3,2,0,1:T(8,128)S(1)} %get-tuple-element.15, f32[4,8,8,1]{3,2,0,1:T(8,128)S(1)} %get-tuple-element.13, ...), kind=kLoop, calls=%fused_computation.30 | loop fusion | flops 655360 | bytes 1703936 | tf_op jit(solution)/shard_map/sub | solution.py:29
  14.3 3.7 %all-to-all-start = ((f32[4,8,8,256]{3,2,0,1:T(8,128)}), f32[4,8,8,256]{3,2,0,1:T(8,128)S(1)}, u32[]{:S(2)}, u32[]{:S(2)}) async-start(f32[4,8,8,256]{3,2,0,1:T(8,128)} %fusion.13), calls=%async_computation | async-start | bytes 524288 | tf_op jit(solution)/shard_map/all_to_all | solution.py:85
  18.0 0.7 %compare_and_fusion = pred[8,128]{1,0:T(8,128)(4,1)S(1)} fusion(s32[64,128]{1,0:T(8,128)} %bitcast.88, s32[]{:T(128)S(6)} %select_n.18), kind=kLoop, calls=%fused_computation.73 | loop fusion | flops 6144 | bytes 5124 | tf_op jit(solution)/shard_map/vmap(jit(_take))/and | solution.py:64
  18.7 6.2 %all-to-all-done = f32[4,8,8,256]{3,2,0,1:T(8,128)S(1)} async-done(((f32[4,8,8,256]{3,2,0,1:T(8,128)}), f32[4,8,8,256]{3,2,0,1:T(8,128)S(1)}, u32[]{:S(2)}, u32[]{:S(2)}) %all-to-all-start) | async-done | bytes 262176 | tf_op jit(solution)/shard_map/all_to_all | solution.py:85
  24.9 0.4 copy.19
  25.3 6.8 %gather_fusion = f32[1024,32]{1,0:T(8,128)S(1)} fusion(f32[8,32,256]{1,2,0:T(8,128)S(1)} %bitcast.74, s32[1024]{0:T(1024)S(1)} %fusion.37), kind=kCustom, calls=%fused_computation | custom fusion | bytes 270336 | tf_op jit(solution)/shard_map/vmap(jit(_take))/gather | solution.py:64
  32.1 0.2 copy.20
  32.3 0.7 %subtract_multiply_fusion = (f32[8,128]{1,0:T(8,128)S(1)}, f32[8,128]{1,0:T(8,128)S(1)}, f32[8,128]{1,0:T(8,128)S(1)}) fusion(f32[64,128]{1,0:T(8,128)} %bitcast.89, s32[]{:T(128)S(6)} %select_n.18, f32[64,128]{1,0:T(8,128)} %bitcast.90, f32[8,128]{1,0:T(8,128)S(1)} %bitcast_reduce_fusion.1), kind=kLoop, calls=%fused_computation.71 | loop fusion | flops 3072 | bytes 24580 | tf_op jit(solution)/shard_map/mul | solution.py:54
  33.0 0.4 multiply_reduce_fusion
  33.4 0.3 fusion.3
  33.8 0.3 fusion.33
  34.1 0.3 fusion.28
  34.4 0.3 fusion.2
  34.6 0.3 fusion.46
  34.9 0.3 fusion.45
  35.2 0.3 convolution_bitcast_fusion
  35.5 0.3 fusion.1
  35.7 0.3 convolution_divide_fusion
  36.0 0.3 fusion.47
  36.3 0.3 fusion.48
  36.7 0.5 %fusion = f32[32,1,8,256]{3,0,2,1:T(8,128)S(1)} fusion(f32[32,8,256]{2,1,0:T(8,128)S(1)} %broadcast_subtract_fusion, f32[8,32,32]{2,1,0:T(8,128)S(1)} %convolution_divide_fusion, f32[8,256]{1,0:T(8,128)S(1)} %broadcast_multiply_fusion, f32[8,32]{1,0:T(8,128)S(1)} %bitcast.85), kind=kOutput, calls=%fused_computation.2 | convolution fusion | flops 25247744 | bytes 566272 | tf_op jit(solution)/shard_map/rkm,krn->mrn/dot_general | solution.py:59
  37.2 0.2 copy.23
  37.3 9.3 %all_to_all.33 = f32[32,1,8,256]{3,2,1,0:T(8,128)S(1)} all-to-all(f32[32,1,8,256]{3,2,1,0:T(8,128)S(1)} %copy.23), channel_id=1, replica_groups=mesh['member'=8,'lat'=4] {'member'}, dimensions={0} | all-to-all | bytes 524288 | tf_op jit(solution)/shard_map/all_to_all | solution.py:94
  46.7 0.7 %copy.41 = f32[8,4,1,8,256]{4,3,0,1,2:T(8,128)} copy(f32[8,4,1,8,256]{4,3,1,0,2:T(8,128)S(1)} %bitcast.83) | data formatting | bytes 524288 | tf_op jit(solution)/shard_map/all_to_all | solution.py:94
  (10 shorter events, 0.2 us)
Async XLA Ops:
  0.0 12.5 %copy-start = (f32[4,8,8,256]{3,2,1,0:T(8,128)S(1)}, f32[4,8,8,256]{3,2,1,0:T(8,128)}, u32[]{:S(2)}) copy-start(f32[4,8,8,256]{3,2,1,0:T(8,128)} %param.6) | copy-start | bytes 786436
  0.0 12.5 %copy-start.1 = (f32[8,8,256]{2,1,0:T(8,128)S(1)}, f32[8,8,256]{2,1,0:T(8,128)}, u32[]{:S(2)}) copy-start(f32[8,8,256]{2,1,0:T(8,128)} %param.8) | copy-start | bytes 196612
  0.0 12.5 %copy-start.2 = (f32[8,8,256]{2,1,0:T(8,128)S(1)}, f32[8,8,256]{2,1,0:T(8,128)}, u32[]{:S(2)}) copy-start(f32[8,8,256]{2,1,0:T(8,128)} %param.7) | copy-start | bytes 196612
  1.0 7.2 %collective-permute-start = (f32[6,2,8,256]{3,2,0,1:T(8,128)S(1)}, f32[6,2,8,256]{3,2,0,1:T(8,128)S(1)}, u32[]{:S(2)}, u32[]{:S(2)}) collective-permute-start(f32[6,2,8,256]{3,2,0,1:T(8,128)S(1)} %get-tuple-element.12), channel_id=1, source_target_pairs={{0,1},{1,2},{2,3},{4,5},{5,6},{6,7},{8,9},{9,10},{10,11},{12,13},{... | collective-permute-start | bytes 294920 | tf_op jit(solution)/shard_map/ppermute | solution.py:15
  6.0 6.5 %collective-permute-start.1 = (f32[6,2,8,256]{3,2,0,1:T(8,128)S(1)}, f32[6,2,8,256]{3,2,0,1:T(8,128)S(1)}, u32[]{:S(2)}, u32[]{:S(2)}) collective-permute-start(f32[6,2,8,256]{3,2,0,1:T(8,128)S(1)} %get-tuple-element.11), channel_id=1, source_target_pairs={{1,0},{2,1},{3,2},{5,4},{6,5},{7,6},{9,8},{10,9},{11,10},{13,12},{... | collective-permute-start | bytes 294920 | tf_op jit(solution)/shard_map/ppermute | solution.py:18
  14.3 10.6 %all-to-all-start = ((f32[4,8,8,256]{3,2,0,1:T(8,128)}), f32[4,8,8,256]{3,2,0,1:T(8,128)S(1)}, u32[]{:S(2)}, u32[]{:S(2)}) async-start(f32[4,8,8,256]{3,2,0,1:T(8,128)} %fusion.13), calls=%async_computation | async-start | bytes 524288 | tf_op jit(solution)/shard_map/all_to_all | solution.py:85
where the time goes:
time: 47.8 us; the launch traced here: 47.4 us
  waiting for transfers between devices  10.7 us (22%)
  starting transfers between devices  9.98 us (21%)
  blocking collectives  9.32 us (19%)
  local copies, waits for them, and re-layouts  8.71 us (18%)
  other arithmetic  4.47 us (9%)
  matrix products  4.01 us (8%)
    all_to_all x1, blocking collectives, body(): lax.all_to_all(analysed.reshape(count, 1, regions, longitudes), 'member',...  9.32 us
    gather x2, local copies, waits for them, and re-layouts, pick_columns(): jnp.take(block, index, axis=1)  6.96 us
    all_to_all x1, waiting for transfers between devices, body(): lax.all_to_all(flat.reshape(members_dev, groups, regions, longitudes), 'm...  6.19 us
    ppermute x1, starting transfers between devices, extended_2(): lax.ppermute(lax.slice_in_dim(block, block.shape[dim] - width, None, axis...  4.97 us
    ppermute x1, waiting for transfers between devices, extended_2(): lax.ppermute(lax.slice_in_dim(block, 0, width, axis=dim), axis, backward)  4.32 us
    all_to_all x1, starting transfers between devices, body(): lax.all_to_all(flat.reshape(members_dev, groups, regions, longitudes), 'm...  3.72 us
    ppermute x1, starting transfers between devices, extended_2(): lax.ppermute(lax.slice_in_dim(block, 0, width, axis=dim), axis, backward)  1.29 us
    sub x2, other arithmetic, advance(): middle - step_size * ((zonal + middle) * (east_cell - west_cell) * 0.5 +...  1.16 us
  transfers between devices with their start and end apart: 3, of which 3 were waited for; matrix products, arithmetic and copies ran while one was open for 3% of the time, Pallas kernels for 0%

commit v1 on v0

--- a/solution.py
+++ b/solution.py
@@ -82,12 +82,20 @@
     cells = lax.dynamic_slice_in_dim(all_cells, start, regions, 0)
     values = lax.dynamic_slice_in_dim(obs_value.reshape(lat_dev * levels, -1), start, regions, 0)
     weights = lax.dynamic_slice_in_dim(obs_weight.reshape(lat_dev * levels, -1), start, regions, 0)
-    ensemble = lax.all_to_all(
-        flat.reshape(members_dev, groups, regions, longitudes),
-        "member",
-        split_axis=1,
-        concat_axis=0,
-        tiled=True,
+    ensemble = jnp.concatenate(
+        lax.all_to_all(
+            jnp.stack(
+                jnp.split(
+                    flat.reshape(members_dev, groups, regions, longitudes),
+                    lax.axis_size("member"),
+                    axis=1,
+                )
+            ),
+            "member",
+            0,
+            0,
+        ),
+        axis=0,
     ).reshape(count, regions, longitudes)
     observed = pick_columns(ensemble, cells)
     analysed = analyse(ensemble, observed, values, weights)

time: 47.8 us -> 52 us (1.088)
  local copies, waits for them, and re-layouts: 8.71 us -> 13.6 us
  other arithmetic: 4.47 us -> 3.75 us
    unnamed x6 -> x13, local copies, waits for them, and re-layouts: 0.01 us -> 4.33 us
    another operation x0 -> x2, local copies, waits for them, and re-layouts: none -> 0.98 us  [the longest x1 0.62 us: body(): jnp.stack(jnp.split(flat.reshape(members_dev, groups, regions, longitudes...]
    sub x2, other arithmetic: 1.16 us -> 0.44 us  [advance(): middle - step_size * ((zonal + middle) * (east_cell - west_cell) * 0.5 +...]
where the time goes in v1:
time: 52 us; the launch traced here: 51.6 us
  local copies, waits for them, and re-layouts  13.6 us (26%)
  waiting for transfers between devices  10.7 us (21%)
  starting transfers between devices  9.98 us (19%)
  blocking collectives  9.32 us (18%)
  matrix products  4 us (8%)
  other arithmetic  3.75 us (7%)
    all_to_all x1, blocking collectives, body(): lax.all_to_all(analysed.reshape(count, 1, regions, longitudes), 'member',...  9.32 us
    gather x2, local copies, waits for them, and re-layouts, pick_columns(): jnp.take(block, index, axis=1)  6.96 us
    all_to_all x1, waiting for transfers between devices, body(): lax.all_to_all(jnp.stack(jnp.split(flat.reshape(members_dev, groups, regi...  6.19 us
    ppermute x1, starting transfers between devices, extended_2(): lax.ppermute(lax.slice_in_dim(block, block.shape[dim] - width, None, axis...  4.97 us
    unnamed x13, local copies, waits for them, and re-layouts  4.33 us
    ppermute x1, waiting for transfers between devices, extended_2(): lax.ppermute(lax.slice_in_dim(block, 0, width, axis=dim), axis, backward)  4.32 us
    all_to_all x1, starting transfers between devices, body(): lax.all_to_all(jnp.stack(jnp.split(flat.reshape(members_dev, groups, regi...  3.72 us
    ppermute x1, starting transfers between devices, extended_2(): lax.ppermute(lax.slice_in_dim(block, 0, width, axis=dim), axis, backward)  1.29 us
  transfers between devices with their start and end apart: 3, of which 3 were waited for; matrix products, arithmetic and copies ran while one was open for 3% of the time, Pallas kernels for 0%

profile of v1, /device:TPU:0, one launch (start us, length us, event | category | flops | bytes accessed | tf_op | source)
XLA Modules:
  0.0 51.6 jit_solution(10878212042118664636)
XLA Ops:
  0.0 0.0 copy-start
  0.0 0.0 copy-start.1
  0.0 0.0 copy-start.2
  0.0 1.0 %pad_maximum_fusion.7 = (f32[6,2,8,256]{3,2,0,1:T(8,128)S(1)}, f32[6,2,8,256]{3,2,0,1:T(8,128)S(1)}) fusion(f32[1,8,8,256]{3,2,0,1:T(8,128)} %bitcast.102, f32[1,8,8,256]{3,2,0,1:T(8,128)} %bitcast.106, f32[4,8,8,256]{3,2,1,0:T(8,128)} %param.6), kind=kLoop, calls=%fused_computation.44 | loop fusion | flops 98304 | bytes 589824 | tf_op jit(solution)/shard_map/concatenate | solution.py:73
  1.0 5.0 %collective-permute-start = (f32[6,2,8,256]{3,2,0,1:T(8,128)S(1)}, f32[6,2,8,256]{3,2,0,1:T(8,128)S(1)}, u32[]{:S(2)}, u32[]{:S(2)}) collective-permute-start(f32[6,2,8,256]{3,2,0,1:T(8,128)S(1)} %get-tuple-element.12), channel_id=1, source_target_pairs={{0,1},{1,2},{2,3},{4,5},{5,6},{6,7},{8,9},{9,10},{10,11},{12,13},{... | collective-permute-start | bytes 294920 | tf_op jit(solution)/shard_map/ppermute | solution.py:15
  6.0 1.3 %collective-permute-start.1 = (f32[6,2,8,256]{3,2,0,1:T(8,128)S(1)}, f32[6,2,8,256]{3,2,0,1:T(8,128)S(1)}, u32[]{:S(2)}, u32[]{:S(2)}) collective-permute-start(f32[6,2,8,256]{3,2,0,1:T(8,128)S(1)} %get-tuple-element.11), channel_id=1, source_target_pairs={{1,0},{2,1},{3,2},{5,4},{6,5},{7,6},{9,8},{10,9},{11,10},{13,12},{... | collective-permute-start | bytes 294920 | tf_op jit(solution)/shard_map/ppermute | solution.py:18
  7.3 0.7 %fusion.45 = s32[1024]{0:T(1024)S(1)} fusion(s32[64,128]{1,0:T(8,128)} %bitcast.114, s32[]{:T(128)S(6)} %select_n.18), kind=kLoop, calls=%fused_computation.85 | loop fusion | flops 8192 | bytes 8196 | tf_op jit(solution)/shard_map/vmap(jit(_take))/gather | solution.py:64
  8.0 0.2 collective-permute-done
  8.2 4.3 %collective-permute-done.1 = f32[6,2,8,256]{3,2,0,1:T(8,128)S(1)} collective-permute-done((f32[6,2,8,256]{3,2,0,1:T(8,128)S(1)}, f32[6,2,8,256]{3,2,0,1:T(8,128)S(1)}, u32[]{:S(2)}, u32[]{:S(2)}) %collective-permute-start.1) | collective-permute-done | bytes 98336 | tf_op jit(solution)/shard_map/ppermute | solution.py:18
  12.5 0.0 copy-done
  12.5 0.0 copy-done.1
  12.5 0.0 copy-done.2
  12.6 0.2 fusion.50
  12.7 0.1 fusion.49
  12.9 0.2 fusion.8
  13.1 0.1 fusion.52
  13.3 0.1 fusion.51
  13.4 0.2 fusion.13
  13.6 0.6 %fusion.40 = f32[8,4,1,8,256]{4,3,1,2,0:T(8,128)} fusion(f32[4,8,8,256]{3,2,0,1:T(8,128)S(1)} %fusion.13), kind=kLoop, calls=%fused_computation.77 | loop fusion | bytes 65536
  14.2 0.6 %fusion.39 = f32[8,4,1,8,256]{4,3,1,2,0:T(8,128)} fusion(f32[8,4,1,8,256]{4,3,1,2,0:T(8,128)} %fusion.40, f32[4,8,8,256]{3,2,0,1:T(8,128)S(1)} %fusion.13), kind=kLoop, calls=%fused_computation.75 | loop fusion | bytes 65536
  14.8 0.6 %fusion.38 = f32[8,4,1,8,256]{4,3,1,2,0:T(8,128)} fusion(f32[8,4,1,8,256]{4,3,1,2,0:T(8,128)} %fusion.39, f32[4,8,8,256]{3,2,0,1:T(8,128)S(1)} %fusion.13), kind=kLoop, calls=%fused_computation.73 | loop fusion | bytes 65536
  15.4 0.6 %fusion.37 = f32[8,4,1,8,256]{4,3,1,2,0:T(8,128)} fusion(f32[8,4,1,8,256]{4,3,1,2,0:T(8,128)} %fusion.38, f32[4,8,8,256]{3,2,0,1:T(8,128)S(1)} %fusion.13), kind=kLoop, calls=%fused_computation.71 | loop fusion | bytes 65536
  16.0 0.6 %fusion.36 = f32[8,4,1,8,256]{4,3,1,2,0:T(8,128)} fusion(f32[8,4,1,8,256]{4,3,1,2,0:T(8,128)} %fusion.37, f32[4,8,8,256]{3,2,0,1:T(8,128)S(1)} %fusion.13), kind=kLoop, calls=%fused_computation.69 | loop fusion | bytes 65536
  16.6 0.6 %fusion.35 = f32[8,4,1,8,256]{4,3,1,2,0:T(8,128)} fusion(f32[8,4,1,8,256]{4,3,1,2,0:T(8,128)} %fusion.36, f32[4,8,8,256]{3,2,0,1:T(8,128)S(1)} %fusion.13), kind=kLoop, calls=%fused_computation.67 | loop fusion | bytes 65536
  17.3 0.6 %fusion.34 = f32[8,4,1,8,256]{4,3,1,2,0:T(8,128)} fusion(f32[8,4,1,8,256]{4,3,1,2,0:T(8,128)} %fusion.35, f32[4,8,8,256]{3,2,0,1:T(8,128)S(1)} %fusion.13), kind=kLoop, calls=%fused_computation.65 | loop fusion | bytes 65536
  17.9 0.6 %fusion.33 = f32[8,4,1,8,256]{4,3,1,2,0:T(8,128)} fusion(f32[8,4,1,8,256]{4,3,1,2,0:T(8,128)} %fusion.34, f32[4,8,8,256]{3,2,0,1:T(8,128)S(1)} %fusion.13), kind=kLoop, calls=%fused_computation.63 | loop fusion | bytes 65536 | tf_op jit(solution)/shard_map/stack | solution.py:87
  18.5 3.7 %all-to-all-start = ((f32[8,4,1,8,256]{4,3,1,2,0:T(8,128)}), f32[8,4,1,8,256]{4,3,1,2,0:T(8,128)S(1)}, u32[]{:S(2)}, u32[]{:S(2)}) async-start(f32[8,4,1,8,256]{4,3,1,2,0:T(8,128)} %fusion.33), calls=%async_computation | async-start | bytes 524288 | tf_op jit(solution)/shard_map/all_to_all | solution.py:86
  22.2 0.7 %compare_and_fusion = pred[8,128]{1,0:T(8,128)(4,1)S(1)} fusion(s32[64,128]{1,0:T(8,128)} %bitcast.115, s32[]{:T(128)S(6)} %select_n.18), kind=kLoop, calls=%fused_computation.88 | loop fusion | flops 6144 | bytes 5124 | tf_op jit(solution)/shard_map/vmap(jit(_take))/and | solution.py:64
  22.9 6.2 %all-to-all-done = f32[8,4,1,8,256]{4,3,1,2,0:T(8,128)S(1)} async-done(((f32[8,4,1,8,256]{4,3,1,2,0:T(8,128)}), f32[8,4,1,8,256]{4,3,1,2,0:T(8,128)S(1)}, u32[]{:S(2)}, u32[]{:S(2)}) %all-to-all-start) | async-done | bytes 262176 | tf_op jit(solution)/shard_map/all_to_all | solution.py:86
  29.1 0.4 copy.33
  29.5 6.8 %gather_fusion = f32[1024,32]{1,0:T(8,128)S(1)} fusion(f32[8,32,256]{1,2,0:T(8,128)S(1)} %bitcast.101, s32[1024]{0:T(1024)S(1)} %fusion.45), kind=kCustom, calls=%fused_computation | custom fusion | bytes 270336 | tf_op jit(solution)/shard_map/vmap(jit(_take))/gather | solution.py:64
  36.3 0.2 copy.34
  36.5 0.7 %subtract_multiply_fusion = (f32[8,128]{1,0:T(8,128)S(1)}, f32[8,128]{1,0:T(8,128)S(1)}, f32[8,128]{1,0:T(8,128)S(1)}) fusion(f32[64,128]{1,0:T(8,128)} %bitcast.116, s32[]{:T(128)S(6)} %select_n.18, f32[64,128]{1,0:T(8,128)} %bitcast.117, f32[8,128]{1,0:T(8,128)S(1)} %bitcast_reduce_fusion), kind=kLoop, calls=%fused_computation.86 | loop fusion | flops 3072 | bytes 24580 | tf_op jit(solution)/shard_map/mul | solution.py:54
  37.2 0.4 multiply_reduce_fusion
  37.7 0.3 fusion.3
  38.0 0.3 fusion.41
  38.3 0.3 fusion.28
  38.6 0.3 fusion.2
  38.9 0.3 fusion.54
  39.1 0.3 fusion.53
  39.4 0.3 convolution_bitcast_fusion
  39.7 0.3 fusion.1
  40.0 0.3 convolution_divide_fusion
  40.2 0.3 fusion.55
  40.5 0.3 fusion.56
  40.9 0.5 fusion
  41.4 0.2 copy.37
  41.6 9.3 %all_to_all.23 = f32[32,1,8,256]{3,2,1,0:T(8,128)S(1)} all-to-all(f32[32,1,8,256]{3,2,1,0:T(8,128)S(1)} %copy.37), channel_id=1, replica_groups=mesh['member'=8,'lat'=4] {'member'}, dimensions={0} | all-to-all | bytes 524288 | tf_op jit(solution)/shard_map/all_to_all | solution.py:102
  50.9 0.7 %copy.55 = f32[8,4,1,8,256]{4,3,0,1,2:T(8,128)} copy(f32[8,4,1,8,256]{4,3,1,0,2:T(8,128)S(1)} %bitcast.110) | data formatting | bytes 524288 | tf_op jit(solution)/shard_map/all_to_all | solution.py:102
  (10 shorter events, 0.2 us)
Async XLA Ops:
  0.0 12.5 %copy-start = (f32[4,8,8,256]{3,2,1,0:T(8,128)S(1)}, f32[4,8,8,256]{3,2,1,0:T(8,128)}, u32[]{:S(2)}) copy-start(f32[4,8,8,256]{3,2,1,0:T(8,128)} %param.6) | copy-start | bytes 786436
  0.0 12.5 %copy-start.1 = (f32[8,8,256]{2,1,0:T(8,128)S(1)}, f32[8,8,256]{2,1,0:T(8,128)}, u32[]{:S(2)}) copy-start(f32[8,8,256]{2,1,0:T(8,128)} %param.8) | copy-start | bytes 196612
  0.0 12.5 %copy-start.2 = (f32[8,8,256]{2,1,0:T(8,128)S(1)}, f32[8,8,256]{2,1,0:T(8,128)}, u32[]{:S(2)}) copy-start(f32[8,8,256]{2,1,0:T(8,128)} %param.7) | copy-start | bytes 196612
  1.0 7.2 %collective-permute-start = (f32[6,2,8,256]{3,2,0,1:T(8,128)S(1)}, f32[6,2,8,256]{3,2,0,1:T(8,128)S(1)}, u32[]{:S(2)}, u32[]{:S(2)}) collective-permute-start(f32[6,2,8,256]{3,2,0,1:T(8,128)S(1)} %get-tuple-element.12), channel_id=1, source_target_pairs={{0,1},{1,2},{2,3},{4,5},{5,6},{6,7},{8,9},{9,10},{10,11},{12,13},{... | collective-permute-start | bytes 294920 | tf_op jit(solution)/shard_map/ppermute | solution.py:15
  6.0 6.5 %collective-permute-start.1 = (f32[6,2,8,256]{3,2,0,1:T(8,128)S(1)}, f32[6,2,8,256]{3,2,0,1:T(8,128)S(1)}, u32[]{:S(2)}, u32[]{:S(2)}) collective-permute-start(f32[6,2,8,256]{3,2,0,1:T(8,128)S(1)} %get-tuple-element.11), channel_id=1, source_target_pairs={{1,0},{2,1},{3,2},{5,4},{6,5},{7,6},{9,8},{10,9},{11,10},{13,12},{... | collective-permute-start | bytes 294920 | tf_op jit(solution)/shard_map/ppermute | solution.py:18
  18.5 10.6 %all-to-all-start = ((f32[8,4,1,8,256]{4,3,1,2,0:T(8,128)}), f32[8,4,1,8,256]{4,3,1,2,0:T(8,128)S(1)}, u32[]{:S(2)}, u32[]{:S(2)}) async-start(f32[8,4,1,8,256]{4,3,1,2,0:T(8,128)} %fusion.33), calls=%async_computation | async-start | bytes 524288 | tf_op jit(solution)/shard_map/all_to_all | solution.py:86
